TPU v7x, 256 devices: a whole 4x4x8 slice. The times are simulated.
256 devices in a mesh: dp: 32 (over y, x, core), shard: 8 (over z).
Axes of the slice: x: 4, y: 4, z: 8, core: 2. Of those that a mesh axis runs over, the one named last changes fastest.
Arguments:
- grads: bfloat16 [2, 32, 4096, 4096], P(None, 'dp', 'shard'), may hold values from -0.5 to 0.5
- basis: float32 [2, 4096, 256], P(None, 'shard'), may hold values from -0.375 to 0.375
- weight: float32 [2, 8, 32, 16, 4096], P(None, 'shard', 'dp'), may hold values from -6 to 6
- moment_m: float32 [2, 4096, 256], P(None, 'dp'), may hold values from -6 to 6
- moment_v: float32 [2, 4096, 256], P(None, 'dp'), may hold values from 0.25 to 4
Outputs:
- new_weight: float32 [2, 8, 32, 16, 4096], P(None, 'shard', 'dp')
- new_m: float32 [2, 4096, 256], P(None, 'dp')
- new_v: float32 [2, 4096, 256], P(None, 'dp')
- new_basis: float32 [2, 4096, 256], P(None, 'shard')
All inputs are finite; a program needn't handle non-finite values.
Results may differ from a plain program's by a relative error of at most 0.0036.
Values may be sent and summed in bfloat16 or wider, within the bound.
A program may use at most 64 MiB of HBM per device.

v0:
```python
import jax
import jax.numpy as jnp
from jax import lax
from jax.sharding import PartitionSpec as P

MATS = 2
NS_STEPS = 5


def adam_step(moment_m, moment_v, projected):
    next_m = 0.9 * moment_m + 0.1 * projected
    next_v = 0.999 * moment_v + 0.001 * projected * projected
    update = 2.0 * (next_m / (1.0 - 0.9**10)) / (jnp.sqrt(next_v / (1.0 - 0.999**10)) + 1e-08)
    return (next_m, next_v, update)


def ns_turn(iterate, gram):
    return 1.5 * iterate - 0.5 * jnp.dot(iterate, gram, precision=lax.Precision.HIGHEST)


def shards(grads, basis, weight, moment_m, moment_v):
    group_index = lax.axis_index("dp")
    rows_weight = weight.shape[3]
    weights_out, firsts, seconds, bases = ([], [], [], [])
    for matrix in range(MATS):
        gradient = grads[matrix, 0]
        basis_local = basis[matrix]
        basis_bf = basis_local.astype(jnp.bfloat16)
        partial_sum = lax.psum_scatter(
            lax.dot_general(
                gradient, basis_bf, (((0,), (0,)), ((), ())), preferred_element_type=jnp.float32
            ),
            "dp",
            scatter_dimension=0,
            tiled=True,
        )
        projected = lax.psum(partial_sum, "shard")
        next_m, next_v, update = adam_step(moment_m[matrix], moment_v[matrix], projected)
        full_update = lax.all_gather(update, "dp", axis=0, tiled=True)
        basis_rows = lax.dynamic_slice_in_dim(
            basis_local, group_index * rows_weight, rows_weight, 0
        )
        delta = jnp.dot(basis_rows, full_update.T, precision=lax.Precision.HIGHEST)
        weights_out.append((weight[matrix, 0, 0] - delta).reshape(weight.shape[1:]))
        projected_bf = projected.astype(jnp.bfloat16)
        refresh_part = jnp.dot(
            gradient,
            lax.all_gather(projected_bf, "dp", axis=0, tiled=True),
            preferred_element_type=jnp.float32,
        )
        refresh = lax.psum(refresh_part, "dp")
        total_sq = lax.psum(jnp.sum(refresh * refresh), "shard")
        iterate = refresh / jnp.sqrt(total_sq + 1e-06)
        first_turn = 0
        for step in range(first_turn, NS_STEPS):
            gram = lax.psum(
                jnp.dot(iterate.T, iterate, precision=lax.Precision.HIGHEST).astype(jnp.bfloat16),
                "shard",
            ).astype(jnp.float32)
            iterate = ns_turn(iterate, gram)
        bases.append(iterate)
        firsts.append(next_m)
        seconds.append(next_v)
    return (jnp.stack(weights_out), jnp.stack(firsts), jnp.stack(seconds), jnp.stack(bases))


def solution(mesh):
    placed = (
        P(None, "dp", "shard", None),
        P(None, "shard", None),
        P(None, "shard", "dp", None, None),
        P(None, "dp", None),
        P(None, "dp", None),
    )
    return jax.shard_map(
        shards,
        mesh=mesh,
        in_specs=placed,
        out_specs=(
            P(None, "shard", "dp", None, None),
            P(None, "dp", None),
            P(None, "dp", None),
            P(None, "shard", None),
        ),
        check_vma=False,
    )
```

profile of v0, /device:TPU:1, one launch (start us, length us, event | category | flops | bytes accessed | tf_op | source)
XLA Modules:
  0.0 1018.5 jit_solution(8599303258596466312)
XLA Ops:
  7.2 5.5 fusion.4
  14.0 5.5 fusion.8
  19.6 85.4 %reduce-scatter.5.cloned.1.call-done = f32[128,256]{1,0:T(8,128)} async-done(((f32[4096,256]{1,0:T(8,128)}), f32[128,256]{1,0:T(8,128)}) %reduce-scatter.5.cloned.1.call-update) | async-done | bytes 131088 | tf_op jit(solution)/shard_map/reduce_scatter | solution.py:29
  104.9 93.3 %reduce-scatter.3.cloned.1.call-done = f32[128,256]{1,0:T(8,128)} async-done(((f32[4096,256]{1,0:T(8,128)}), f32[128,256]{1,0:T(8,128)}) %reduce-scatter.3.cloned.1.call-update) | async-done | bytes 131088 | tf_op jit(solution)/shard_map/reduce_scatter | solution.py:29
  198.3 71.4 %all-reduce.18.cloned.1.call-done = (f32[128,256]{1,0:T(8,128)}, f32[128,256]{1,0:T(8,128)}) async-done(((f32[128,256]{1,0:T(8,128)}, f32[128,256]{1,0:T(8,128)}), (f32[128,256]{1,0:T(8,128)}, f32[128,256]{1,0:T(8,128)})) %all-reduce.18.cloned.1.call-update) | async-done | bytes 262160 | tf_op jit(solution)/shard_map/psum | solution.py:37
  269.8 2.0 add_divide_fusion.1
  272.4 52.9 %all-gather.9.cloned.1.call-done = bf16[4096,256]{1,0:T(8,128)(2,1)} async-done(((bf16[128,256]{1,0:T(8,128)(2,1)}), bf16[4096,256]{1,0:T(8,128)(2,1)}) %all-gather.9.cloned.1.call-update) | async-done | bytes 2097168 | tf_op jit(solution)/shard_map/all_gather | solution.py:48
  325.3 4.9 fusion.14
  330.2 46.1 %all-gather.11.cloned.1.call-done = bf16[4096,256]{1,0:T(8,128)(2,1)} async-done(((bf16[128,256]{1,0:T(8,128)(2,1)}), bf16[4096,256]{1,0:T(8,128)(2,1)}) %all-gather.11.cloned.1.call-update) | async-done | bytes 2097168 | tf_op jit(solution)/shard_map/all_gather | solution.py:48
  376.3 4.9 fusion.17
  381.3 114.6 %all-reduce.16.cloned.1.call-done = (f32[512,256]{0,1:T(8,128)}, f32[512,256]{0,1:T(8,128)}) async-done(((f32[512,256]{0,1:T(8,128)}, f32[512,256]{0,1:T(8,128)}), (f32[512,256]{0,1:T(8,128)}, f32[512,256]{0,1:T(8,128)})) %all-reduce.16.cloned.1.call-update) | async-done | bytes 1048592 | tf_op jit(solution)/shard_map/psum | solution.py:51
  495.8 2.0 multiply_reduce_fusion
  497.8 14.3 %all-reduce.1 = (f32[]{:T(128)}, f32[]{:T(128)}) all-reduce(f32[]{:T(128)} %get-tuple-element.36, f32[]{:T(128)} %get-tuple-element.37), channel_id=1, replica_groups=mesh['dp'=32,'shard'=8] {'shard'}, use_global_device_ids=true, to_apply=%region_14.0 | all-reduce | flops 2 | bytes 16 | tf_op jit(solution)/shard_map/psum | solution.py:52
  513.5 2.5 convolution_convert_fusion.4
  516.1 2.5 convolution_convert_fusion.9
  518.6 68.6 %all-reduce.28.cloned.1.call-done = (bf16[256,256]{1,0:T(8,128)(2,1)}, bf16[256,256]{1,0:T(8,128)(2,1)}) async-done(((bf16[256,256]{1,0:T(8,128)(2,1)}, bf16[256,256]{1,0:T(8,128)(2,1)}), (bf16[256,256]{1,0:T(8,128)(2,1)}, bf16[256,256]{1,0:T(8,128)(2,1)})) %all-reduce.28.cloned.1.call-update) | async-done | bytes 262160 | tf_op jit(solution)/shard_map/psum | solution.py:56
  592.8 71.3 %all-reduce.26.cloned.1.call-done = (bf16[256,256]{1,0:T(8,128)(2,1)}, bf16[256,256]{1,0:T(8,128)(2,1)}) async-done(((bf16[256,256]{1,0:T(8,128)(2,1)}, bf16[256,256]{1,0:T(8,128)(2,1)}), (bf16[256,256]{1,0:T(8,128)(2,1)}, bf16[256,256]{1,0:T(8,128)(2,1)})) %all-reduce.26.cloned.1.call-update) | async-done | bytes 262160 | tf_op jit(solution)/shard_map/psum | solution.py:56
  669.6 71.5 %all-reduce.24.cloned.1.call-done = (bf16[256,256]{1,0:T(8,128)(2,1)}, bf16[256,256]{1,0:T(8,128)(2,1)}) async-done(((bf16[256,256]{1,0:T(8,128)(2,1)}, bf16[256,256]{1,0:T(8,128)(2,1)}), (bf16[256,256]{1,0:T(8,128)(2,1)}, bf16[256,256]{1,0:T(8,128)(2,1)})) %all-reduce.24.cloned.1.call-update) | async-done | bytes 262160 | tf_op jit(solution)/shard_map/psum | solution.py:56
  746.5 71.5 %all-reduce.22.cloned.1.call-done = (bf16[256,256]{1,0:T(8,128)(2,1)}, bf16[256,256]{1,0:T(8,128)(2,1)}) async-done(((bf16[256,256]{1,0:T(8,128)(2,1)}, bf16[256,256]{1,0:T(8,128)(2,1)}), (bf16[256,256]{1,0:T(8,128)(2,1)}, bf16[256,256]{1,0:T(8,128)(2,1)})) %all-reduce.22.cloned.1.call-update) | async-done | bytes 262160 | tf_op jit(solution)/shard_map/psum | solution.py:56
  826.8 68.2 %all-reduce.20.cloned.1.call-done = (bf16[256,256]{1,0:T(8,128)(2,1)}, bf16[256,256]{1,0:T(8,128)(2,1)}) async-done(((bf16[256,256]{1,0:T(8,128)(2,1)}, bf16[256,256]{1,0:T(8,128)(2,1)}), (bf16[256,256]{1,0:T(8,128)(2,1)}, bf16[256,256]{1,0:T(8,128)(2,1)})) %all-reduce.20.cloned.1.call-update) | async-done | bytes 262160 | tf_op jit(solution)/shard_map/psum | solution.py:56
  899.2 53.3 %all-gather.5.cloned.1.call-done = f32[4096,256]{1,0:T(8,128)} async-done(((f32[128,256]{1,0:T(8,128)}), f32[4096,256]{1,0:T(8,128)}) %all-gather.5.cloned.1.call-update) | async-done | bytes 4194320 | tf_op jit(solution)/shard_map/all_gather | solution.py:39
  952.4 5.7 fusion.1
  958.1 47.4 %all-gather.7.cloned.1.call-done = f32[4096,256]{1,0:T(8,128)} async-done(((f32[128,256]{1,0:T(8,128)}), f32[4096,256]{1,0:T(8,128)}) %all-gather.7.cloned.1.call-update) | async-done | bytes 4194320 | tf_op jit(solution)/shard_map/all_gather | solution.py:39
  1005.5 5.7 fusion
  (61 shorter events, 32.2 us)
Async XLA Ops:
  7.2 97.8 %reduce-scatter.5.cloned.1.call-start = ((), (), s32[]{:S(2)}) async-start(), calls=%async_computation.4 | async-start | bytes 4325376 | tf_op jit(solution)/shard_map/reduce_scatter | solution.py:29
  12.8 1.2 copy-start
  12.8 185.5 %reduce-scatter.3.cloned.1.call-start = ((), (), s32[]{:S(2)}) async-start(), calls=%async_computation.2 | async-start | bytes 4325376 | tf_op jit(solution)/shard_map/reduce_scatter | solution.py:29
  19.5 250.3 %copy-start.4 = (f32[2,128,256]{2,1,0:T(8,128)S(1)}, f32[2,128,256]{2,1,0:T(8,128)}, u32[]{:S(2)}) copy-start(f32[2,128,256]{2,1,0:T(8,128)} %param.8) | copy-start | bytes 786436
  19.5 250.3 %copy-start.5 = (f32[2,128,256]{2,1,0:T(8,128)S(1)}, f32[2,128,256]{2,1,0:T(8,128)}, u32[]{:S(2)}) copy-start(f32[2,128,256]{2,1,0:T(8,128)} %param.9) | copy-start | bytes 786436
  19.5 250.2 %all-reduce.18.cloned.1.call-start = ((), (), s32[]{:S(2)}) async-start(), calls=%async_computation.9 | async-start | bytes 524288 | tf_op jit(solution)/shard_map/psum | solution.py:37
  198.3 127.0 %all-gather.9.cloned.1.call-start = ((), (), s32[]{:S(2)}) async-start(), calls=%async_computation.6 | async-start | bytes 2162688 | tf_op jit(solution)/shard_map/all_gather | solution.py:48
  271.7 104.5 %all-gather.11.cloned.1.call-start = ((), (), s32[]{:S(2)}) async-start(), calls=%async_computation.7 | async-start | bytes 2162688 | tf_op jit(solution)/shard_map/all_gather | solution.py:48
  272.3 223.5 %all-reduce.16.cloned.1.call-start = ((), (), s32[]{:S(2)}) async-start(), calls=%async_computation.8 | async-start | bytes 2097152 | tf_op jit(solution)/shard_map/psum | solution.py:51
  381.2 206.0 %all-reduce.28.cloned.1.call-start = ((), (), s32[]{:S(2)}) async-start(), calls=%async_computation.14 | async-start | bytes 524288 | tf_op jit(solution)/shard_map/psum | solution.py:56
  495.8 91.4 %copy-start.3 = (f32[512,256]{0,1:T(8,128)S(1)}, f32[512,256]{0,1:T(8,128)}, u32[]{:S(2)}) copy-start(f32[512,256]{0,1:T(8,128)} %get-tuple-element.9) | copy-start | bytes 1572868
  497.8 90.8 %copy-start.2 = (f32[512,256]{0,1:T(8,128)S(1)}, f32[512,256]{0,1:T(8,128)}, u32[]{:S(2)}) copy-start(f32[512,256]{0,1:T(8,128)} %get-tuple-element.8) | copy-start | bytes 1572868
  518.6 145.6 %all-reduce.26.cloned.1.call-start = ((), (), s32[]{:S(2)}) async-start(), calls=%async_computation.13 | async-start | bytes 524288 | tf_op jit(solution)/shard_map/psum | solution.py:56
  592.6 148.5 %all-reduce.24.cloned.1.call-start = ((), (), s32[]{:S(2)}) async-start(), calls=%async_computation.12 | async-start | bytes 524288 | tf_op jit(solution)/shard_map/psum | solution.py:56
  669.5 148.5 %all-reduce.22.cloned.1.call-start = ((), (), s32[]{:S(2)}) async-start(), calls=%async_computation.11 | async-start | bytes 524288 | tf_op jit(solution)/shard_map/psum | solution.py:56
  746.4 148.5 %all-reduce.20.cloned.1.call-start = ((), (), s32[]{:S(2)}) async-start(), calls=%async_computation.10 | async-start | bytes 524288 | tf_op jit(solution)/shard_map/psum | solution.py:56
  823.3 129.1 %all-gather.5.cloned.1.call-start = ((), (), s32[]{:S(2)}) async-start(), calls=%async_computation.3 | async-start | bytes 4325376 | tf_op jit(solution)/shard_map/all_gather | solution.py:39
  823.9 181.6 %all-gather.7.cloned.1.call-start = ((), (), s32[]{:S(2)}) async-start(), calls=%async_computation.5 | async-start | bytes 4325376 | tf_op jit(solution)/shard_map/all_gather | solution.py:39
  825.9 126.5 %copy-start.1 = (f32[2,1,1,16,4096]{4,3,2,1,0:T(8,128)S(1)}, f32[2,1,1,16,4096]{4,3,2,1,0:T(8,128)}, u32[]{:S(2)}) copy-start(f32[2,1,1,16,4096]{4,3,2,1,0:T(8,128)} %param.7) | copy-start | bytes 1572868
Sparse Core Ops, SparseCore 0:
  12.9 91.9 reduce-scatter.4
  108.9 89.3 reduce-scatter.2
  200.6 69.0 all-reduce.17
  272.7 52.5 all-gather.8
  328.3 47.9 all-gather.10
  381.3 114.4 all-reduce.15
  518.7 68.4 all-reduce.27
  592.7 71.3 all-reduce.25
  669.6 71.3 all-reduce.23
  746.5 71.3 all-reduce.21
  823.5 71.4 all-reduce.19
  897.4 54.9 all-gather.4
  955.0 50.4 all-gather.6
where the time goes:
time: 1020 us
  waiting for transfers between devices  917 us (90%)
  matrix products  61.3 us (6%)
  between operations  15.4 us (2%)
  blocking collectives  14.3 us (1%)
    psum x5, waiting for transfers between devices, shards(): lax.psum(jnp.dot(iterate.T, iterate, precision=lax.Precision.HIGHEST).ast...  351 us
    reduce_scatter x2, waiting for transfers between devices, shards(): lax.psum_scatter(lax.dot_general(gradient, basis_bf, (((0,), (0,)), ((),...  179 us
    psum x1, waiting for transfers between devices, shards(): refresh = lax.psum(refresh_part, 'dp')  115 us
    all_gather x2, waiting for transfers between devices, shards(): full_update = lax.all_gather(update, 'dp', axis=0, tiled=True)  101 us
    all_gather x2, waiting for transfers between devices, shards(): lax.all_gather(projected_bf, 'dp', axis=0, tiled=True)  99 us
    psum x1, waiting for transfers between devices, shards(): projected = lax.psum(partial_sum, 'shard')  71.4 us
  transfers between devices with their start and end apart: 13, of which 13 were waited for; matrix products, arithmetic and copies ran while one was open for 2% of the time, Pallas kernels for 0%

commit v1 on v0

--- a/solution.py
+++ b/solution.py
@@ -45,7 +45,9 @@
         projected_bf = projected.astype(jnp.bfloat16)
         refresh_part = jnp.dot(
             gradient,
-            lax.all_gather(projected_bf, "dp", axis=0, tiled=True),
+            jnp.concatenate(
+                lax.all_to_all(jnp.stack([projected_bf] * lax.axis_size("dp")), "dp", 0, 0), axis=0
+            ),
             preferred_element_type=jnp.float32,
         )
         refresh = lax.psum(refresh_part, "dp")

time: 1020 us -> 986 us (0.967)
  waiting for transfers between devices: 917 us -> 838 us
  blocking collectives: 14.3 us -> 55.2 us
    all_gather x2 -> x0, waiting for transfers between devices: 99 us -> none  [shards(): lax.all_gather(projected_bf, 'dp', axis=0, tiled=True)]
    all_to_all x0 -> x1, blocking collectives: none -> 40.9 us  [shards(): lax.all_to_all(jnp.stack([projected_bf] * lax.axis_size('dp')), 'dp', 0, 0)]
    all_to_all x0 -> x1, waiting for transfers between devices: none -> 23.3 us  [shards(): lax.all_to_all(jnp.stack([projected_bf] * lax.axis_size('dp')), 'dp', 0, 0)]
  transfers between devices with their start and end apart: 13 -> 12, of which waited for: 13 -> 12; matrix products, arithmetic and copies ran while one was open for 2% -> 2% of each run, Pallas kernels for 0% -> 0%
where the time goes in v1:
time: 986 us; the launch traced here: 985 us
  waiting for transfers between devices  838 us (85%)
  matrix products  60.6 us (6%)
  blocking collectives  55.2 us (6%)
  between operations  15.4 us (2%)
    psum x5, waiting for transfers between devices, shards(): lax.psum(jnp.dot(iterate.T, iterate, precision=lax.Precision.HIGHEST).ast...  351 us
    reduce_scatter x2, waiting for transfers between devices, shards(): lax.psum_scatter(lax.dot_general(gradient, basis_bf, (((0,), (0,)), ((),...  179 us
    psum x1, waiting for transfers between devices, shards(): refresh = lax.psum(refresh_part, 'dp')  111 us
    all_gather x2, waiting for transfers between devices, shards(): full_update = lax.all_gather(update, 'dp', axis=0, tiled=True)  101 us
    psum x1, waiting for transfers between devices, shards(): projected = lax.psum(partial_sum, 'shard')  71.5 us
    all_to_all x1, blocking collectives, shards(): lax.all_to_all(jnp.stack([projected_bf] * lax.axis_size('dp')), 'dp', 0, 0)  40.9 us
    all_to_all x1, waiting for transfers between devices, shards(): lax.all_to_all(jnp.stack([projected_bf] * lax.axis_size('dp')), 'dp', 0, 0)  23.3 us
  transfers between devices with their start and end apart: 12, of which 12 were waited for; matrix products, arithmetic and copies ran while one was open for 2% of the time, Pallas kernels for 0%

profile of v1, /device:TPU:1, one launch (start us, length us, event | category | flops | bytes accessed | tf_op | source)
XLA Modules:
  0.0 985.4 jit_solution(14126825464938857118)
XLA Ops:
  7.2 5.5 fusion.4
  14.0 5.5 fusion.8
  19.5 85.4 %reduce-scatter.5.cloned.1.call-done = f32[128,256]{1,0:T(8,128)} async-done(((f32[4096,256]{1,0:T(8,128)}), f32[128,256]{1,0:T(8,128)}) %reduce-scatter.5.cloned.1.call-update) | async-done | bytes 131088 | tf_op jit(solution)/shard_map/reduce_scatter | solution.py:29
  104.9 93.3 %reduce-scatter.3.cloned.1.call-done = f32[128,256]{1,0:T(8,128)} async-done(((f32[4096,256]{1,0:T(8,128)}), f32[128,256]{1,0:T(8,128)}) %reduce-scatter.3.cloned.1.call-update) | async-done | bytes 131088 | tf_op jit(solution)/shard_map/reduce_scatter | solution.py:29
  198.3 71.5 %all-reduce.18.cloned.1.call-done = (f32[128,256]{1,0:T(8,128)}, f32[128,256]{1,0:T(8,128)}) async-done(((f32[128,256]{1,0:T(8,128)}, f32[128,256]{1,0:T(8,128)}), (f32[128,256]{1,0:T(8,128)}, f32[128,256]{1,0:T(8,128)})) %all-reduce.18.cloned.1.call-update) | async-done | bytes 262160 | tf_op jit(solution)/shard_map/psum | solution.py:37
  272.0 40.9 %all_to_all.10 = bf16[32,128,256]{2,1,0:T(8,128)(2,1)} all-to-all(bf16[32,128,256]{2,1,0:T(8,128)(2,1)S(1)} %stack.31), channel_id=1, replica_groups=mesh['dp'=32,'shard'=8] {'dp'}, dimensions={0} | all-to-all | bytes 4194304 | tf_op jit(solution)/shard_map/all_to_all | solution.py:49
  314.4 4.1 all-to-all-start.1
  318.6 4.9 fusion.14
  323.5 23.3 %all-to-all-done.1 = bf16[32,128,256]{2,1,0:T(8,128)(2,1)S(1)} async-done(((bf16[32,128,256]{2,1,0:T(8,128)(2,1)}), bf16[32,128,256]{2,1,0:T(8,128)(2,1)S(1)}, u32[]{:S(2)}, u32[]{:S(2)}) %all-to-all-start.1) | async-done | bytes 2097184 | tf_op jit(solution)/shard_map/all_to_all | solution.py:49
  346.8 4.3 fusion.17
  351.2 111.4 %all-reduce.16.cloned.1.call-done = (f32[512,256]{0,1:T(8,128)}, f32[512,256]{0,1:T(8,128)}) async-done(((f32[512,256]{0,1:T(8,128)}, f32[512,256]{0,1:T(8,128)}), (f32[512,256]{0,1:T(8,128)}, f32[512,256]{0,1:T(8,128)})) %all-reduce.16.cloned.1.call-update) | async-done | bytes 1048592 | tf_op jit(solution)/shard_map/psum | solution.py:53
  462.5 2.0 multiply_reduce_fusion
  464.5 14.3 %all-reduce.1 = (f32[]{:T(128)}, f32[]{:T(128)}) all-reduce(f32[]{:T(128)} %get-tuple-element.36, f32[]{:T(128)} %get-tuple-element.37), channel_id=1, replica_groups=mesh['dp'=32,'shard'=8] {'shard'}, use_global_device_ids=true, to_apply=%region_14.0 | all-reduce | flops 2 | bytes 16 | tf_op jit(solution)/shard_map/psum | solution.py:54
  480.2 2.5 convolution_convert_fusion.4
  482.8 2.5 convolution_convert_fusion.9
  485.3 68.6 %all-reduce.28.cloned.1.call-done = (bf16[256,256]{1,0:T(8,128)(2,1)}, bf16[256,256]{1,0:T(8,128)(2,1)}) async-done(((bf16[256,256]{1,0:T(8,128)(2,1)}, bf16[256,256]{1,0:T(8,128)(2,1)}), (bf16[256,256]{1,0:T(8,128)(2,1)}, bf16[256,256]{1,0:T(8,128)(2,1)})) %all-reduce.28.cloned.1.call-update) | async-done | bytes 262160 | tf_op jit(solution)/shard_map/psum | solution.py:58
  559.5 71.4 %all-reduce.26.cloned.1.call-done = (bf16[256,256]{1,0:T(8,128)(2,1)}, bf16[256,256]{1,0:T(8,128)(2,1)}) async-done(((bf16[256,256]{1,0:T(8,128)(2,1)}, bf16[256,256]{1,0:T(8,128)(2,1)}), (bf16[256,256]{1,0:T(8,128)(2,1)}, bf16[256,256]{1,0:T(8,128)(2,1)})) %all-reduce.26.cloned.1.call-update) | async-done | bytes 262160 | tf_op jit(solution)/shard_map/psum | solution.py:58
  636.4 71.6 %all-reduce.24.cloned.1.call-done = (bf16[256,256]{1,0:T(8,128)(2,1)}, bf16[256,256]{1,0:T(8,128)(2,1)}) async-done(((bf16[256,256]{1,0:T(8,128)(2,1)}, bf16[256,256]{1,0:T(8,128)(2,1)}), (bf16[256,256]{1,0:T(8,128)(2,1)}, bf16[256,256]{1,0:T(8,128)(2,1)})) %all-reduce.24.cloned.1.call-update) | async-done | bytes 262160 | tf_op jit(solution)/shard_map/psum | solution.py:58
  713.3 71.5 %all-reduce.22.cloned.1.call-done = (bf16[256,256]{1,0:T(8,128)(2,1)}, bf16[256,256]{1,0:T(8,128)(2,1)}) async-done(((bf16[256,256]{1,0:T(8,128)(2,1)}, bf16[256,256]{1,0:T(8,128)(2,1)}), (bf16[256,256]{1,0:T(8,128)(2,1)}, bf16[256,256]{1,0:T(8,128)(2,1)})) %all-reduce.22.cloned.1.call-update) | async-done | bytes 262160 | tf_op jit(solution)/shard_map/psum | solution.py:58
  793.7 68.2 %all-reduce.20.cloned.1.call-done = (bf16[256,256]{1,0:T(8,128)(2,1)}, bf16[256,256]{1,0:T(8,128)(2,1)}) async-done(((bf16[256,256]{1,0:T(8,128)(2,1)}, bf16[256,256]{1,0:T(8,128)(2,1)}), (bf16[256,256]{1,0:T(8,128)(2,1)}, bf16[256,256]{1,0:T(8,128)(2,1)})) %all-reduce.20.cloned.1.call-update) | async-done | bytes 262160 | tf_op jit(solution)/shard_map/psum | solution.py:58
  866.0 53.3 %all-gather.3.cloned.1.call-done = f32[4096,256]{1,0:T(8,128)} async-done(((f32[128,256]{1,0:T(8,128)}), f32[4096,256]{1,0:T(8,128)}) %all-gather.3.cloned.1.call-update) | async-done | bytes 4194320 | tf_op jit(solution)/shard_map/all_gather | solution.py:39
  919.3 5.7 fusion.1
  924.9 47.4 %all-gather.5.cloned.1.call-done = f32[4096,256]{1,0:T(8,128)} async-done(((f32[128,256]{1,0:T(8,128)}), f32[4096,256]{1,0:T(8,128)}) %all-gather.5.cloned.1.call-update) | async-done | bytes 4194320 | tf_op jit(solution)/shard_map/all_gather | solution.py:39
  972.4 5.7 fusion
  (60 shorter events, 35.4 us)
Async XLA Ops:
  7.2 97.8 %reduce-scatter.5.cloned.1.call-start = ((), (), s32[]{:S(2)}) async-start(), calls=%async_computation.6 | async-start | bytes 4325376 | tf_op jit(solution)/shard_map/reduce_scatter | solution.py:29
  12.8 1.2 copy-start
  12.8 185.5 %reduce-scatter.3.cloned.1.call-start = ((), (), s32[]{:S(2)}) async-start(), calls=%async_computation.4 | async-start | bytes 4325376 | tf_op jit(solution)/shard_map/reduce_scatter | solution.py:29
  19.5 250.3 %copy-start.4 = (f32[2,128,256]{2,1,0:T(8,128)S(1)}, f32[2,128,256]{2,1,0:T(8,128)}, u32[]{:S(2)}) copy-start(f32[2,128,256]{2,1,0:T(8,128)} %param.8) | copy-start | bytes 786436
  19.5 250.3 %copy-start.5 = (f32[2,128,256]{2,1,0:T(8,128)S(1)}, f32[2,128,256]{2,1,0:T(8,128)}, u32[]{:S(2)}) copy-start(f32[2,128,256]{2,1,0:T(8,128)} %param.9) | copy-start | bytes 786436
  19.5 250.3 %all-reduce.18.cloned.1.call-start = ((), (), s32[]{:S(2)}) async-start(), calls=%async_computation.9 | async-start | bytes 524288 | tf_op jit(solution)/shard_map/psum | solution.py:37
  314.4 32.4 %all-to-all-start.1 = ((bf16[32,128,256]{2,1,0:T(8,128)(2,1)}), bf16[32,128,256]{2,1,0:T(8,128)(2,1)S(1)}, u32[]{:S(2)}, u32[]{:S(2)}) async-start(bf16[32,128,256]{2,1,0:T(8,128)(2,1)} %stack.33), calls=%async_computation.3 | async-start | bytes 4194304 | tf_op jit(solution)/shard_map/all_to_all | solution.py:49
  318.5 144.0 %all-reduce.16.cloned.1.call-start = ((), (), s32[]{:S(2)}) async-start(), calls=%async_computation.8 | async-start | bytes 2097152 | tf_op jit(solution)/shard_map/psum | solution.py:53
  351.1 202.8 %all-reduce.28.cloned.1.call-start = ((), (), s32[]{:S(2)}) async-start(), calls=%async_computation.14 | async-start | bytes 524288 | tf_op jit(solution)/shard_map/psum | solution.py:58
  462.5 91.4 %copy-start.3 = (f32[512,256]{0,1:T(8,128)S(1)}, f32[512,256]{0,1:T(8,128)}, u32[]{:S(2)}) copy-start(f32[512,256]{0,1:T(8,128)} %get-tuple-element.9) | copy-start | bytes 1572868
  464.5 90.8 %copy-start.2 = (f32[512,256]{0,1:T(8,128)S(1)}, f32[512,256]{0,1:T(8,128)}, u32[]{:S(2)}) copy-start(f32[512,256]{0,1:T(8,128)} %get-tuple-element.8) | copy-start | bytes 1572868
  485.3 145.7 %all-reduce.26.cloned.1.call-start = ((), (), s32[]{:S(2)}) async-start(), calls=%async_computation.13 | async-start | bytes 524288 | tf_op jit(solution)/shard_map/psum | solution.py:58
  559.3 148.6 %all-reduce.24.cloned.1.call-start = ((), (), s32[]{:S(2)}) async-start(), calls=%async_computation.12 | async-start | bytes 524288 | tf_op jit(solution)/shard_map/psum | solution.py:58
  636.3 148.5 %all-reduce.22.cloned.1.call-start = ((), (), s32[]{:S(2)}) async-start(), calls=%async_computation.11 | async-start | bytes 524288 | tf_op jit(solution)/shard_map/psum | solution.py:58
  713.3 148.6 %all-reduce.20.cloned.1.call-start = ((), (), s32[]{:S(2)}) async-start(), calls=%async_computation.10 | async-start | bytes 524288 | tf_op jit(solution)/shard_map/psum | solution.py:58
  790.2 129.1 %all-gather.3.cloned.1.call-start = ((), (), s32[]{:S(2)}) async-start(), calls=%async_computation.5 | async-start | bytes 4325376 | tf_op jit(solution)/shard_map/all_gather | solution.py:39
  790.8 181.6 %all-gather.5.cloned.1.call-start = ((), (), s32[]{:S(2)}) async-start(), calls=%async_computation.7 | async-start | bytes 4325376 | tf_op jit(solution)/shard_map/all_gather | solution.py:39
  792.8 126.5 %copy-start.1 = (f32[2,1,1,16,4096]{4,3,2,1,0:T(8,128)S(1)}, f32[2,1,1,16,4096]{4,3,2,1,0:T(8,128)}, u32[]{:S(2)}) copy-start(f32[2,1,1,16,4096]{4,3,2,1,0:T(8,128)} %param.7) | copy-start | bytes 1572868
Sparse Core Ops, SparseCore 0:
  12.9 91.9 reduce-scatter.4
  108.9 89.3 reduce-scatter.2
  200.6 69.0 all-reduce.17
  351.2 111.2 all-reduce.15
  485.4 68.4 all-reduce.27
  559.4 71.4 all-reduce.25
  636.4 71.4 all-reduce.23
  713.4 71.3 all-reduce.21
  790.3 71.4 all-reduce.19
  864.3 54.9 all-gather.2
  921.8 50.4 all-gather.4
